TPU v7x, 256 devices: a whole 4x4x8 slice. The times are simulated.
256 devices in a mesh: seq: 32 (over x, y, core), head: 8 (over z).
Axes of the slice: x: 4, y: 4, z: 8, core: 2. Of those that a mesh axis runs over, the one named last changes fastest.
Arguments:
- positions: int32 [16384], P('seq'), may hold values from 65535 to 98301, as said below
- queries: bfloat16 [16384, 32, 128], P('seq', 'head'), may hold values from -16 to 16
- keys: bfloat16 [16384, 16, 128], P('seq', 'head'), may hold values from -16 to 16
- values: bfloat16 [16384, 16, 128], P('seq', 'head'), may hold values from -6 to 6
- out_weight: bfloat16 [4096, 5376], P('head', 'seq'), may hold values from -0.1875 to 0.1875
- post_gain: float32 [5376], P('head'), may hold values from 0.25 to 1.75
- residual: bfloat16 [16384, 5376], P('seq', 'head'), may hold values from -6 to 6
Outputs:
- layer_out: bfloat16 [16384, 5376], P('seq', 'head')
Inputs may be any that keep to these rules, and one draw needn't show every extreme that they name: `positions`: strictly rising, by 1 or 2 from one token to the next; the last token's position is the most.
All inputs are finite; a program needn't handle non-finite values.
Results may differ from a plain program's by a relative error of at most 0.015.
Values may be sent and summed in bfloat16 or wider, within the bound.
No kernel may reach another device: no remote copies, remote signals or barrier semaphores. Data moves between devices by JAX's collectives and lax.ppermute only.
A program may use at most 64 MiB of HBM per device.

v0:
```python
import jax
import jax.numpy as jnp
from jax import lax
from jax.sharding import PartitionSpec as P

D = 5376
QUERY_HEADS = 32
KEY_VALUE_HEADS = 16
VISIBLE_SPAN = 1024
EPS = 1e-06
SCALE = 168.0 ** (-0.5)


def passed_along(value, axis, steps):
    count = lax.axis_size(axis)
    initial, last = (max(0, -steps), min(count, count - steps))
    return lax.ppermute(value, axis, [(source, source + steps) for source in range(initial, last)])


def copy_for_each(array, axis):
    length = lax.axis_size(axis)
    return lax.all_to_all(
        jnp.broadcast_to(array[None], (length, *array.shape)), axis, 0, 0, tiled=True
    )


def of_everyone(array, axis):
    return copy_for_each(array, axis).sum(axis=0)


def rotate(x, positions):
    half = x.shape[-1] // 2
    inverse = 10000.0 ** (-2.0 * jnp.arange(half, dtype=jnp.float32) / x.shape[-1])
    angle = positions.astype(jnp.float32)[:, None] * inverse[None, :]
    cosine = jnp.concatenate([jnp.cos(angle), jnp.cos(angle)], -1)[:, None, :]
    sine = jnp.concatenate([jnp.sin(angle), jnp.sin(angle)], -1)[:, None, :]
    source = x.astype(jnp.float32)
    turned = jnp.concatenate([-source[..., half:], source[..., :half]], -1)
    return (source * cosine + turned * sine).astype(jnp.bfloat16)


def on_device(positions, queries, keys, values, out_weight, post_gain, residual):
    rows = queries.shape[0]
    kv_heads = keys.shape[1]
    query_groups = QUERY_HEADS // KEY_VALUE_HEADS
    q_rot = rotate(queries, positions)
    stacked = jnp.stack([rotate(keys, positions), values], 0)
    reach = (VISIBLE_SPAN + rows - 2) // rows
    pieces = []
    carried = stacked
    for hop in range(reach):
        carried = passed_along(carried, "seq", 1)
        pieces.insert(0, carried)
    extended = jnp.concatenate(pieces + [stacked], axis=1)
    extra = extended.shape[1] - rows
    anchor = lax.axis_index("seq") * rows
    block_length = min(512, rows)
    query_tile_rows = q_rot.reshape(block_length, kv_heads, query_groups, -1)
    key_block = extended[0, 0 : extra + block_length]
    value_block = extended[1, 0 : extra + block_length]
    scores = (
        jnp.einsum("qhgd,khd->hgqk", query_tile_rows, key_block, preferred_element_type=jnp.float32)
        * SCALE
    )
    query_index = anchor + 0 + jnp.arange(block_length, dtype=jnp.int32)
    key_index = anchor - extra + 0 + jnp.arange(extra + block_length, dtype=jnp.int32)
    gap = query_index[:, None] - key_index[None, :]
    allowed = (gap >= 0) & (gap < VISIBLE_SPAN) & (key_index[None, :] >= 0)
    scores = jnp.where(allowed, scores, -1e30)
    top = jnp.max(scores, axis=-1, keepdims=True)
    weights = jnp.exp(scores - top)
    probs = (weights / jnp.sum(weights, axis=-1, keepdims=True)).astype(jnp.bfloat16)
    context = jnp.einsum("hgqk,khd->qhgd", probs, value_block, preferred_element_type=jnp.float32)
    outputs = context.astype(jnp.bfloat16).reshape(block_length, -1)
    context = outputs
    partial_value = jnp.dot(
        context,
        lax.all_gather(out_weight, "seq", axis=1, tiled=True),
        preferred_element_type=jnp.float32,
    )
    attended = lax.psum_scatter(
        partial_value.astype(jnp.bfloat16), "head", scatter_dimension=1, tiled=True
    ).astype(jnp.float32)
    squares = of_everyone(jnp.sum(attended * attended, axis=1), "head")
    scaled = attended * lax.rsqrt(squares / D + EPS)[:, None]
    result = residual.astype(jnp.float32) + post_gain[None, :] * scaled
    return result.astype(jnp.bfloat16)


def solution(mesh):
    return jax.shard_map(
        on_device,
        mesh=mesh,
        in_specs=(
            P("seq"),
            P("seq", "head", None),
            P("seq", "head", None),
            P("seq", "head", None),
            P("head", "seq"),
            P("head"),
            P("seq", "head"),
        ),
        out_specs=P("seq", "head"),
        check_vma=False,
    )
```

profile of v0, /device:TPU:2, one launch (start us, length us, event | category | flops | bytes accessed | tf_op | source)
XLA Modules:
  0.0 164.7 jit_solution(17591090239701363710)
XLA Ops:
  6.5 0.0 copy-start.3
  6.5 0.0 all-gather.2.cloned.1.call-start
  6.5 0.7 all-gather.2.cloned.1.call-update
  7.3 0.0 reduce-scatter.2.cloned.1.call-start
  7.3 0.7 convert_element_type.39
  8.0 1.0 copy.44
  9.0 1.0 multiply_cosine_fusion
  10.0 0.2 pad_maximum_fusion.1
  10.2 0.0 copy-start
  10.2 1.0 copy_convert_fusion
  11.3 0.2 slice_negate_fusion.1
  11.5 0.0 copy-done.3
  11.5 0.2 fusion.24
  11.7 0.0 copy-start.1
  11.7 0.9 pad_maximum_fusion
  12.6 1.9 %collective-permute-start = (bf16[2,512,2,128]{3,1,2,0:T(8,128)(2,1)}, bf16[2,512,2,128]{3,1,2,0:T(8,128)(2,1)}, u32[]{:S(2)}, u32[]{:S(2)}) collective-permute-start(bf16[2,512,2,128]{3,1,2,0:T(8,128)(2,1)} %pad_maximum_fusion), channel_id=1, source_target_pairs={{0,8},{8,16},{16,24},{24,32},{32,40},{40,48},{48,56},{56,64},{64,7... | collective-permute-start | bytes 1572872 | tf_op jit(solution)/shard_map/ppermute | solution.py:17
  14.5 0.0 copy-done.1
  14.5 0.0 copy-done
  14.5 0.1 convert_element_type.41
  14.6 0.1 slice.29
  14.8 0.0 copy-start.2
  14.8 0.6 slice_negate_fusion
  15.4 1.6 fusion.16
  17.1 0.0 copy-start.5
  17.1 8.4 %collective-permute-done = bf16[2,512,2,128]{3,1,2,0:T(8,128)(2,1)} collective-permute-done((bf16[2,512,2,128]{3,1,2,0:T(8,128)(2,1)}, bf16[2,512,2,128]{3,1,2,0:T(8,128)(2,1)}, u32[]{:S(2)}, u32[]{:S(2)}) %collective-permute-start) | collective-permute-done | bytes 524320 | tf_op jit(solution)/shard_map/ppermute | solution.py:17
  25.5 1.9 %collective-permute-start.1 = (bf16[2,512,2,128]{3,1,2,0:T(8,128)(2,1)}, bf16[2,512,2,128]{3,1,2,0:T(8,128)(2,1)S(1)}, u32[]{:S(2)}, u32[]{:S(2)}) collective-permute-start(bf16[2,512,2,128]{3,1,2,0:T(8,128)(2,1)} %collective-permute-done), channel_id=1, source_target_pairs={{0,8},{8,16},{16,24},{24,32},{32,40},{40,48},{48,56},{56,64},{64,7... | collective-permute-start | bytes 1572872 | tf_op jit(solution)/shard_map/ppermute | solution.py:17
  27.4 1.2 fusion.7
  28.6 11.5 %collective-permute-done.1 = bf16[2,512,2,128]{3,1,2,0:T(8,128)(2,1)S(1)} collective-permute-done((bf16[2,512,2,128]{3,1,2,0:T(8,128)(2,1)}, bf16[2,512,2,128]{3,1,2,0:T(8,128)(2,1)S(1)}, u32[]{:S(2)}, u32[]{:S(2)}) %collective-permute-start.1) | collective-permute-done | bytes 524320 | tf_op jit(solution)/shard_map/ppermute | solution.py:17
  40.1 0.0 copy-done.2
  40.1 1.2 maximum_maximum_fusion
  41.3 0.0 copy-done.5
  41.3 7.4 %fusion.27 = (f32[2,2,512]{2,1,0:T(2,128)S(1)}, f32[2,2,512,1536]{2,3,1,0:T(8,128)}) fusion(pred[512,1536]{0,1:T(8,128)(4,1)S(1)} %fusion.7, bf16[2,1536,2,128]{3,1,2,0:T(8,128)(2,1)S(1)} %maximum_maximum_fusion, bf16[512,2,2,128]{3,2,1,0:T(2,128)(2,1)S(1)} %bitcast.46), kind=kOutput, calls=%fused_computation.51 | convolution fusion | flops 817890816 | bytes 14688256 | tf_op jit(solution)/shard_map/sub | solution.py:71
  48.8 6.1 %fusion.14 = bf16[2,128,2,512]{3,1,2,0:T(8,128)(2,1)S(1)} fusion(f32[2,2,512,1536]{2,3,1,0:T(8,128)} %get-tuple-element.10, f32[2,2,512]{2,1,0:T(2,128)S(1)} %get-tuple-element.9, bf16[2,1536,2,128]{3,1,2,0:T(8,128)(2,1)S(1)} %maximum_maximum_fusion), kind=kOutput, calls=%fused_computation.22 | convolution fusion | flops 811859968 | bytes 13901824 | tf_op jit(solution)/shard_map/hgqk,khd->qhgd/dot_general | solution.py:73
  54.9 12.6 %all-gather.2.cloned.1.call-done = bf16[512,5376]{0,1:T(8,128)(2,1)} async-done(((bf16[512,168]{0,1:T(8,128)(2,1)}), bf16[512,5376]{0,1:T(8,128)(2,1)}) %all-gather.2.cloned.1.call-update) | async-done | bytes 5505040 | tf_op jit(solution)/shard_map/all_gather | solution.py:78
  67.4 7.3 %convolution_convert_fusion = bf16[512,5376]{0,1:T(8,128)(2,1)} fusion(bf16[512,5376]{0,1:T(8,128)(2,1)} %all-gather.2.cloned.1.call-done, bf16[512,512]{0,1:T(8,128)(2,1)S(1)} %bitcast.47), kind=kOutput, calls=%fused_computation.5 | convolution fusion | flops 2821324800 | bytes 11534336 | tf_op jit(solution)/shard_map/dot_general | solution.py:76
  74.7 0.0 copy-start.4
  74.7 0.0 copy-start.6
  74.7 0.0 reduce-scatter.2.cloned.1.call-update
  74.8 67.6 %reduce-scatter.2.cloned.1.call-done = bf16[512,672]{0,1:T(8,128)(2,1)} async-done(((bf16[512,5376]{0,1:T(8,128)(2,1)}), bf16[512,672]{0,1:T(8,128)(2,1)}) %reduce-scatter.2.cloned.1.call-update) | async-done | bytes 688144 | tf_op jit(solution)/shard_map/reduce_scatter | solution.py:81
  142.4 1.3 fusion.8
  143.7 11.9 %all_to_all.6 = f32[8,1,512]{2,1,0:T(1,128)S(1)} all-to-all(f32[8,1,512]{2,1,0:T(1,128)S(1)} %broadcast_in_dim.10), channel_id=1, replica_groups=mesh['seq'=32,'head'=8] {'head'}, dimensions={0} | all-to-all | bytes 32768 | tf_op jit(solution)/shard_map/all_to_all | solution.py:22
  155.6 0.0 copy-done.4
  155.7 0.0 copy-done.6
  155.7 2.2 %fusion.11 = bf16[512,672]{0,1:T(8,128)(2,1)} fusion(bf16[512,672]{0,1:T(8,128)(2,1)} %reduce-scatter.2.cloned.1.call-done, bf16[512,672]{0,1:T(8,128)(2,1)S(1)} %copy-done.4, f32[512]{0:T(512)S(1)} %add_rsqrt_fusion, f32[672]{0:T(1024)S(1)} %copy-done.6), kind=kLoop, calls=%fused_computation.20 | loop fusion | flops 2064384 | bytes 2069120 | tf_op jit(solution)/shard_map/convert_element_type | solution.py:87
  (7 shorter events, 0.1 us)
Async XLA Ops:
  6.5 4.9 %copy-start.3 = (bf16[512,2,128]{2,1,0:T(2,128)(2,1)S(1)}, bf16[512,2,128]{2,1,0:T(2,128)(2,1)}, u32[]{:S(2)}) copy-start(bf16[512,2,128]{2,1,0:T(2,128)(2,1)} %param.9) | copy-start | bytes 786436
  6.5 60.9 %all-gather.2.cloned.1.call-start = ((), (), s32[]{:S(2)}) async-start(), calls=%async_computation.2 | async-start | bytes 5677056 | tf_op jit(solution)/shard_map/all_gather | solution.py:78
  7.3 135.1 %reduce-scatter.2.cloned.1.call-start = ((), (), s32[]{:S(2)}) async-start(), calls=%async_computation.3 | async-start | bytes 6193152 | tf_op jit(solution)/shard_map/reduce_scatter | solution.py:81
  10.2 4.3 %copy-start = (bf16[512,4,128]{2,1,0:T(4,128)(2,1)S(1)}, bf16[512,4,128]{2,1,0:T(4,128)(2,1)}, u32[]{:S(2)}) copy-start(bf16[512,4,128]{2,1,0:T(4,128)(2,1)} %param.8) | copy-start | bytes 1572868
  11.7 2.8 %copy-start.1 = (bf16[1,512,2,128]{3,1,2,0:T(8,128)(2,1)}, bf16[1,512,2,128]{3,1,2,0:T(8,128)(2,1)S(1)}, u32[]{:S(2)}) copy-start(bf16[1,512,2,128]{3,1,2,0:T(8,128)(2,1)S(1)} %fusion.24) | copy-start | bytes 786436
  12.6 12.9 %collective-permute-start = (bf16[2,512,2,128]{3,1,2,0:T(8,128)(2,1)}, bf16[2,512,2,128]{3,1,2,0:T(8,128)(2,1)}, u32[]{:S(2)}, u32[]{:S(2)}) collective-permute-start(bf16[2,512,2,128]{3,1,2,0:T(8,128)(2,1)} %pad_maximum_fusion), channel_id=1, source_target_pairs={{0,8},{8,16},{16,24},{24,32},{32,40},{40,48},{48,56},{56,64},{64,7... | collective-permute-start | bytes 1572872 | tf_op jit(solution)/shard_map/ppermute | solution.py:17
  14.8 25.3 %copy-start.2 = (bf16[1,512,2,128]{3,1,2,0:T(8,128)(2,1)S(1)}, bf16[1,512,2,128]{3,1,2,0:T(8,128)(2,1)}, u32[]{:S(2)}) copy-start(bf16[1,512,2,128]{3,1,2,0:T(8,128)(2,1)} %copy-done.1) | copy-start | bytes 786436
  17.1 24.3 %copy-start.5 = (bf16[512,4,128]{2,1,0:T(4,128)(2,1)S(1)}, bf16[512,4,128]{2,1,0:T(4,128)(2,1)}, u32[]{:S(2)}) copy-start(bf16[512,4,128]{2,1,0:T(4,128)(2,1)} %fusion.16) | copy-start | bytes 1572868
  25.5 14.7 %collective-permute-start.1 = (bf16[2,512,2,128]{3,1,2,0:T(8,128)(2,1)}, bf16[2,512,2,128]{3,1,2,0:T(8,128)(2,1)S(1)}, u32[]{:S(2)}, u32[]{:S(2)}) collective-permute-start(bf16[2,512,2,128]{3,1,2,0:T(8,128)(2,1)} %collective-permute-done), channel_id=1, source_target_pairs={{0,8},{8,16},{16,24},{24,32},{32,40},{40,48},{48,56},{56,64},{64,7... | collective-permute-start | bytes 1572872 | tf_op jit(solution)/shard_map/ppermute | solution.py:17
  74.7 80.9 %copy-start.4 = (bf16[512,672]{0,1:T(8,128)(2,1)S(1)}, bf16[512,672]{0,1:T(8,128)(2,1)}, u32[]{:S(2)}) copy-start(bf16[512,672]{0,1:T(8,128)(2,1)} %param.13) | copy-start | bytes 2064388
  74.7 80.9 %copy-start.6 = (f32[672]{0:T(1024)S(1)}, f32[672]{0:T(1024)}, u32[]{:S(2)}) copy-start(f32[672]{0:T(1024)} %param.12) | copy-start | bytes 8068
Sparse Core Ops, SparseCore 0:
  9.9 57.4 all-gather.1
  74.9 67.4 reduce-scatter.1
where the time goes:
time: 165 us
  waiting for transfers between devices  101 us (61%)
  matrix products  20.9 us (13%)
  between operations  13.6 us (8%)
  other arithmetic  12.5 us (8%)
  blocking collectives  11.9 us (7%)
  starting transfers between devices  3.86 us (2%)
    reduce_scatter x1, waiting for transfers between devices, on_device(): lax.psum_scatter(partial_value.astype(jnp.bfloat16), 'head', scatter_dime...  67.6 us
    ppermute x2, waiting for transfers between devices, passed_along(): lax.ppermute(value, axis, [(source, source + steps) for source in range(i...  19.9 us
    all_gather x1, waiting for transfers between devices, on_device(): lax.all_gather(out_weight, 'seq', axis=1, tiled=True)  12.6 us
    all_to_all x1, blocking collectives, copy_for_each(): lax.all_to_all(jnp.broadcast_to(array[None], (length, *array.shape)), axi...  11.9 us
    sub x1, matrix products, on_device(): weights = jnp.exp(scores - top)  7.44 us
    dot_general x1, matrix products, on_device(): jnp.dot(context, lax.all_gather(out_weight, 'seq', axis=1, tiled=True), p...  7.32 us
    dot_general x1, matrix products, on_device(): jnp.einsum('hgqk,khd->qhgd', probs, value_block, preferred_element_type=j...  6.11 us
    ppermute x2, starting transfers between devices, passed_along(): lax.ppermute(value, axis, [(source, source + steps) for source in range(i...  3.82 us
  transfers between devices with their start and end apart: 4, of which 4 were waited for; matrix products, arithmetic and copies ran while one was open for 14% of the time, Pallas kernels for 0%

commit v1 on v0

--- a/solution.py
+++ b/solution.py
@@ -9,6 +9,11 @@
 VISIBLE_SPAN = 1024
 EPS = 1e-06
 SCALE = 168.0 ** (-0.5)
+
+
+def gather_from_all(x, axis, dim):
+    copies = jnp.concatenate([x] * lax.axis_size(axis), axis=dim)
+    return lax.all_to_all(copies, axis, dim, dim, tiled=True)
 
 
 def passed_along(value, axis, steps):
@@ -74,9 +79,7 @@
     outputs = context.astype(jnp.bfloat16).reshape(block_length, -1)
     context = outputs
     partial_value = jnp.dot(
-        context,
-        lax.all_gather(out_weight, "seq", axis=1, tiled=True),
-        preferred_element_type=jnp.float32,
+        context, gather_from_all(out_weight, "seq", 1), preferred_element_type=jnp.float32
     )
     attended = lax.psum_scatter(
         partial_value.astype(jnp.bfloat16), "head", scatter_dimension=1, tiled=True

time: 165 us -> 230 us (1.39)
  waiting for transfers between devices: 101 us -> 144 us
  local copies, waits for them, and re-layouts: 1.14 us -> 17.8 us
  starting transfers between devices: 3.86 us -> 11.8 us
  other arithmetic: 12.5 us -> 10 us
    ppermute x2, waiting for transfers between devices: 19.9 us -> 76.1 us  [passed_along(): lax.ppermute(value, axis, [(source, source + steps) for source in range(i...]
    unnamed x15 -> x52, local copies, waits for them, and re-layouts: 1.01 us -> 17.7 us
    all_gather x1 -> x0, waiting for transfers between devices: 12.6 us -> none  [on_device(): lax.all_gather(out_weight, 'seq', axis=1, tiled=True)]
    all_to_all x0 -> x1, starting transfers between devices: none -> 7.8 us  [gather_from_all(): return lax.all_to_all(copies, axis, dim, dim, tiled=True)]
  transfers between devices with their start and end apart: 4 -> 4, of which waited for: 4 -> 3; matrix products, arithmetic and copies ran while one was open for 14% -> 9% of each run, Pallas kernels for 0% -> 0%
where the time goes in v1:
time: 230 us; the launch traced here: 229 us
  waiting for transfers between devices  144 us (63%)
  matrix products  20.4 us (9%)
  local copies, waits for them, and re-layouts  17.8 us (8%)
  between operations  13.8 us (6%)
  blocking collectives  11.9 us (5%)
  starting transfers between devices  11.8 us (5%)
  other arithmetic  10 us (4%)
    ppermute x2, waiting for transfers between devices, passed_along(): lax.ppermute(value, axis, [(source, source + steps) for source in range(i...  76.1 us
    reduce_scatter x1, waiting for transfers between devices, on_device(): lax.psum_scatter(partial_value.astype(jnp.bfloat16), 'head', scatter_dime...  67.4 us
    unnamed x52, local copies, waits for them, and re-layouts  17.7 us
    all_to_all x1, blocking collectives, copy_for_each(): lax.all_to_all(jnp.broadcast_to(array[None], (length, *array.shape)), axi...  11.9 us
    all_to_all x1, starting transfers between devices, gather_from_all(): return lax.all_to_all(copies, axis, dim, dim, tiled=True)  7.8 us
    sub x1, matrix products, on_device(): weights = jnp.exp(scores - top)  7.45 us
    dot_general x1, matrix products, on_device(): jnp.dot(context, gather_from_all(out_weight, 'seq', 1), preferred_element...  7.33 us
    dot_general x1, matrix products, on_device(): jnp.einsum('hgqk,khd->qhgd', probs, value_block, preferred_element_type=j...  5.66 us
  transfers between devices with their start and end apart: 4, of which 3 were waited for; matrix products, arithmetic and copies ran while one was open for 9% of the time, Pallas kernels for 0%

profile of v1, /device:TPU:2, one launch (start us, length us, event | category | flops | bytes accessed | tf_op | source)
XLA Modules:
  0.0 229.3 jit_solution(11062172207799375831)
XLA Ops:
  6.5 0.0 copy-start
  6.5 1.0 constant_dynamic-update-slice_fusion.31
  7.5 0.9 constant_dynamic-update-slice_fusion.30
  8.5 0.9 constant_dynamic-update-slice_fusion.29
  9.4 0.9 constant_dynamic-update-slice_fusion.28
  10.3 0.9 constant_dynamic-update-slice_fusion.27
  11.3 0.9 constant_dynamic-update-slice_fusion.26
  12.2 0.9 constant_dynamic-update-slice_fusion.25
  13.2 0.9 constant_dynamic-update-slice_fusion.24
  14.1 0.9 constant_dynamic-update-slice_fusion.23
  15.0 0.9 constant_dynamic-update-slice_fusion.22
  16.0 0.9 constant_dynamic-update-slice_fusion.21
  16.9 0.9 constant_dynamic-update-slice_fusion.20
  17.8 0.9 constant_dynamic-update-slice_fusion.19
  18.8 0.9 constant_dynamic-update-slice_fusion.18
  19.7 0.9 constant_dynamic-update-slice_fusion.17
  20.6 0.9 constant_dynamic-update-slice_fusion.16
  21.6 0.0 copy-done
  21.9 0.0 copy-start.2
  21.9 2.4 %copy-done.2 = bf16[512,5376]{0,1:T(8,128)(2,1)} copy-done((bf16[512,5376]{0,1:T(8,128)(2,1)}, bf16[512,5376]{0,1:T(8,128)(2,1)S(1)}, u32[]{:S(2)}) %copy-start.2) | copy-done | bytes 5505048
  24.3 0.0 copy-start.9
  24.3 0.0 copy-start.7
  24.3 0.0 copy-start.5
  24.3 7.8 %all-to-all-start = ((bf16[512,32,168]{0,2,1:T(8,128)(2,1)}), bf16[512,32,168]{0,2,1:T(8,128)(2,1)}, u32[]{:S(2)}, u32[]{:S(2)}) async-start(bf16[512,32,168]{0,2,1:T(8,128)(2,1)} %bitcast.46), calls=%async_computation | async-start | bytes 11010048 | tf_op jit(solution)/shard_map/all_to_all | solution.py:16
  32.1 0.0 copy-start.1
  32.2 0.0 reduce-scatter.2.cloned.1.call-start
  32.2 0.0 copy-done.9
  32.2 1.0 multiply_cosine_fusion
  33.2 0.0 copy-done.7
  33.3 0.2 pad_maximum_fusion.1
  33.5 0.0 copy-done.5
  33.5 0.2 slice_negate_fusion.1
  33.8 0.2 fusion.24
  34.0 0.0 copy-start.3
  34.0 0.9 pad_maximum_fusion
  34.9 2.0 collective-permute-start
  36.9 0.0 copy-done.3
  36.9 0.0 copy-done.1
  36.9 0.1 convert_element_type.41
  37.1 0.1 slice.29
  37.2 0.0 copy-start.4
  37.2 0.6 slice_negate_fusion
  37.8 0.8 fusion.16
  38.7 66.5 %collective-permute-done = bf16[2,512,2,128]{3,1,2,0:T(8,128)(2,1)} collective-permute-done((bf16[2,512,2,128]{3,1,2,0:T(8,128)(2,1)}, bf16[2,512,2,128]{3,1,2,0:T(8,128)(2,1)}, u32[]{:S(2)}, u32[]{:S(2)}) %collective-permute-start) | collective-permute-done | bytes 524320 | tf_op jit(solution)/shard_map/ppermute | solution.py:22
  105.1 1.9 collective-permute-start.1
  107.1 1.2 fusion.7
  108.3 9.7 %collective-permute-done.1 = bf16[2,512,2,128]{3,1,2,0:T(8,128)(2,1)S(1)} collective-permute-done((bf16[2,512,2,128]{3,1,2,0:T(8,128)(2,1)}, bf16[2,512,2,128]{3,1,2,0:T(8,128)(2,1)S(1)}, u32[]{:S(2)}, u32[]{:S(2)}) %collective-permute-start.1) | collective-permute-done | bytes 524320 | tf_op jit(solution)/shard_map/ppermute | solution.py:22
  117.9 0.0 copy-done.4
  117.9 1.2 maximum_maximum_fusion
  119.1 7.4 %fusion.27 = (f32[2,2,512]{2,1,0:T(2,128)S(1)}, f32[2,2,512,1536]{2,3,1,0:T(8,128)}) fusion(pred[512,1536]{0,1:T(8,128)(4,1)S(1)} %fusion.7, bf16[2,1536,2,128]{3,1,2,0:T(8,128)(2,1)S(1)} %maximum_maximum_fusion, bf16[512,2,2,128]{3,2,1,0:T(2,128)(2,1)S(1)} %bitcast.49), kind=kOutput, calls=%fused_computation.83 | convolution fusion | flops 817890816 | bytes 14688256 | tf_op jit(solution)/shard_map/sub | solution.py:76
  126.5 5.7 %fusion.14 = bf16[2,128,2,512]{3,1,2,0:T(8,128)(2,1)S(1)} fusion(f32[2,2,512,1536]{2,3,1,0:T(8,128)} %get-tuple-element.10, f32[2,2,512]{2,1,0:T(2,128)S(1)} %get-tuple-element.9, bf16[2,1536,2,128]{3,1,2,0:T(8,128)(2,1)S(1)} %maximum_maximum_fusion), kind=kOutput, calls=%fused_computation.22 | convolution fusion | flops 811859968 | bytes 13901824 | tf_op jit(solution)/shard_map/hgqk,khd->qhgd/dot_general | solution.py:78
  132.2 0.0 all-to-all-done
  132.2 7.3 %convolution_convert_fusion = bf16[512,5376]{0,1:T(8,128)(2,1)} fusion(bf16[512,5376]{0,1:T(8,128)(2,1)} %bitcast.12, bf16[512,512]{0,1:T(8,128)(2,1)S(1)} %bitcast.50), kind=kOutput, calls=%fused_computation.5 | convolution fusion | flops 2821324800 | bytes 11534336 | tf_op jit(solution)/shard_map/dot_general | solution.py:81
  139.6 0.0 copy-start.6
  139.6 0.0 copy-start.8
  139.6 0.0 reduce-scatter.2.cloned.1.call-update
  139.6 67.4 %reduce-scatter.2.cloned.1.call-done = bf16[512,672]{0,1:T(8,128)(2,1)} async-done(((bf16[512,5376]{0,1:T(8,128)(2,1)}), bf16[512,672]{0,1:T(8,128)(2,1)}) %reduce-scatter.2.cloned.1.call-update) | async-done | bytes 688144 | tf_op jit(solution)/shard_map/reduce_scatter | solution.py:84
  207.0 1.3 fusion.8
  208.3 11.9 %all_to_all.18 = f32[8,1,512]{2,1,0:T(1,128)S(1)} all-to-all(f32[8,1,512]{2,1,0:T(1,128)S(1)} %broadcast_in_dim.10), channel_id=1, replica_groups=mesh['seq'=32,'head'=8] {'head'}, dimensions={0} | all-to-all | bytes 32768 | tf_op jit(solution)/shard_map/all_to_all | solution.py:27
  220.3 0.0 copy-done.6
  220.3 0.0 copy-done.8
  220.3 2.2 fusion.11
  (26 shorter events, 0.4 us)
Async XLA Ops:
  6.5 15.0 %copy-start = (bf16[512,168]{0,1:T(8,128)(2,1)S(1)}, bf16[512,168]{0,1:T(8,128)(2,1)}, u32[]{:S(2)}) copy-start(bf16[512,168]{0,1:T(8,128)(2,1)} %param.11) | copy-start | bytes 516100
  21.9 2.4 %copy-start.2 = (bf16[512,5376]{0,1:T(8,128)(2,1)}, bf16[512,5376]{0,1:T(8,128)(2,1)S(1)}, u32[]{:S(2)}) copy-start(bf16[512,5376]{0,1:T(8,128)(2,1)S(1)} %constant_dynamic-update-slice_fusion) | copy-start | bytes 16515076
  24.3 7.9 %copy-start.9 = (s32[512]{0:T(512)S(1)}, s32[512]{0:T(512)}, u32[]{:S(2)}) copy-start(s32[512]{0:T(512)} %param.7) | copy-start | bytes 6148
  24.3 8.9 %copy-start.7 = (bf16[512,2,128]{2,1,0:T(2,128)(2,1)S(1)}, bf16[512,2,128]{2,1,0:T(2,128)(2,1)}, u32[]{:S(2)}) copy-start(bf16[512,2,128]{2,1,0:T(2,128)(2,1)} %param.10) | copy-start | bytes 786436
  24.3 9.2 %copy-start.5 = (bf16[512,2,128]{2,1,0:T(2,128)(2,1)S(1)}, bf16[512,2,128]{2,1,0:T(2,128)(2,1)}, u32[]{:S(2)}) copy-start(bf16[512,2,128]{2,1,0:T(2,128)(2,1)} %param.9) | copy-start | bytes 786436
  24.3 107.9 %all-to-all-start = ((bf16[512,32,168]{0,2,1:T(8,128)(2,1)}), bf16[512,32,168]{0,2,1:T(8,128)(2,1)}, u32[]{:S(2)}, u32[]{:S(2)}) async-start(bf16[512,32,168]{0,2,1:T(8,128)(2,1)} %bitcast.46), calls=%async_computation | async-start | bytes 11010048 | tf_op jit(solution)/shard_map/all_to_all | solution.py:16
  32.1 4.8 %copy-start.1 = (bf16[512,4,128]{2,1,0:T(4,128)(2,1)S(1)}, bf16[512,4,128]{2,1,0:T(4,128)(2,1)}, u32[]{:S(2)}) copy-start(bf16[512,4,128]{2,1,0:T(4,128)(2,1)} %param.8) | copy-start | bytes 1572868
  32.2 174.8 %reduce-scatter.2.cloned.1.call-start = ((), (), s32[]{:S(2)}) async-start(), calls=%async_computation.3 | async-start | bytes 6193152 | tf_op jit(solution)/shard_map/reduce_scatter | solution.py:84
  34.0 2.9 %copy-start.3 = (bf16[1,512,2,128]{3,1,2,0:T(8,128)(2,1)}, bf16[1,512,2,128]{3,1,2,0:T(8,128)(2,1)S(1)}, u32[]{:S(2)}) copy-start(bf16[1,512,2,128]{3,1,2,0:T(8,128)(2,1)S(1)} %fusion.24) | copy-start | bytes 786436
  34.9 70.3 %collective-permute-start = (bf16[2,512,2,128]{3,1,2,0:T(8,128)(2,1)}, bf16[2,512,2,128]{3,1,2,0:T(8,128)(2,1)}, u32[]{:S(2)}, u32[]{:S(2)}) collective-permute-start(bf16[2,512,2,128]{3,1,2,0:T(8,128)(2,1)} %pad_maximum_fusion), channel_id=1, source_target_pairs={{0,8},{8,16},{16,24},{24,32},{32,40},{40,48},{48,56},{56,64},{64,7... | collective-permute-start | bytes 1572872 | tf_op jit(solution)/shard_map/ppermute | solution.py:22
  37.2 80.8 %copy-start.4 = (bf16[1,512,2,128]{3,1,2,0:T(8,128)(2,1)S(1)}, bf16[1,512,2,128]{3,1,2,0:T(8,128)(2,1)}, u32[]{:S(2)}) copy-start(bf16[1,512,2,128]{3,1,2,0:T(8,128)(2,1)} %copy-done.3) | copy-start | bytes 786436
  105.1 12.8 %collective-permute-start.1 = (bf16[2,512,2,128]{3,1,2,0:T(8,128)(2,1)}, bf16[2,512,2,128]{3,1,2,0:T(8,128)(2,1)S(1)}, u32[]{:S(2)}, u32[]{:S(2)}) collective-permute-start(bf16[2,512,2,128]{3,1,2,0:T(8,128)(2,1)} %collective-permute-done), channel_id=1, source_target_pairs={{0,8},{8,16},{16,24},{24,32},{32,40},{40,48},{48,56},{56,64},{64,7... | collective-permute-start | bytes 1572872 | tf_op jit(solution)/shard_map/ppermute | solution.py:22
  139.6 80.7 %copy-start.6 = (bf16[512,672]{0,1:T(8,128)(2,1)S(1)}, bf16[512,672]{0,1:T(8,128)(2,1)}, u32[]{:S(2)}) copy-start(bf16[512,672]{0,1:T(8,128)(2,1)} %param.13) | copy-start | bytes 2064388
  139.6 80.7 %copy-start.8 = (f32[672]{0:T(1024)S(1)}, f32[672]{0:T(1024)}, u32[]{:S(2)}) copy-start(f32[672]{0:T(1024)} %param.12) | copy-start | bytes 8068
Sparse Core Ops, SparseCore 0:
  139.7 67.2 reduce-scatter.1
